TPU v7x, 256 devices: a whole 4x4x8 slice. The times are simulated.
256 devices in a mesh: row: 16 (over z_hi, y, core), col: 16 (over z_lo, x).
Axes of the slice: x: 4, y: 4, z: 8 (z_hi: 2, z_lo: 4; z = z_hi * 4 + z_lo), core: 2. Of those that a mesh axis runs over, the one named last changes fastest.
Arguments:
- tokens: bfloat16 [2048, 8192], P('col', 'row'), may hold values from -6 to 6
- gate_vals: bfloat16 [448, 64, 4096], P('col', 'row'), may hold values from -0.09375 to 0.09375
- gate_scales: float32 [448, 64], P('col', 'row'), may hold values from 0.3 to 3
- gate_rows: int32 [448, 64], P('col', 'row'), may hold values from 0 to 127, as said below
- up_vals: bfloat16 [448, 64, 4096], P('col', 'row'), may hold values from -0.09375 to 0.09375
- up_scales: float32 [448, 64], P('col', 'row'), may hold values from 0.3 to 3
- up_rows: int32 [448, 64], P('col', 'row'), may hold values from 0 to 127, as said below
- down_vals: bfloat16 [128, 224, 4096], P('row', 'col'), may hold values from -0.046875 to 0.046875
- down_scales: float32 [128, 224], P('row', 'col'), may hold values from 0.3 to 3
- down_rows: int32 [128, 224], P('row', 'col'), may hold values from 0 to 447, as said below
Outputs:
- mixed: bfloat16 [2048, 8192], P('col', 'row')
Inputs may be any that keep to these rules, and one draw needn't show every extreme that they name: Row j of gate_rows holds distinct block rows; slots k with the same k // 4 hold exactly half of the block rows from (k // 4) * 8 to that plus 8 - 1, in increasing order. `up_rows`: same law as gate_rows, drawn independently. Row j of down_rows holds distinct block rows of the hidden units; slots k with the same k // 14 hold exactly half of the block rows from (k // 14) * 28 to that plus 28 - 1, in increasing order.
All inputs are finite; a program needn't handle non-finite values.
Results may differ from a plain program's by a relative error of at most 0.03.
Values may be sent and summed in bfloat16 or wider, within the bound.
A program may use at most 128 MiB of HBM per device.

v0:
```python
import jax
import jax.numpy as jnp
from jax import lax
from jax.sharding import PartitionSpec as P

BLOCK = 64


def dense_panel(values, scales, indices, offset, groups):
    blocks = (values.astype(jnp.float32) * scales[:, :, None]).astype(jnp.bfloat16)
    onehot = (
        indices[:, :, None] - offset == jnp.arange(groups, dtype=jnp.int32)[None, None, :]
    ).astype(jnp.bfloat16)
    matrix = jnp.einsum("jkg,jkc->gjc", onehot, blocks, preferred_element_type=jnp.float32).astype(
        jnp.bfloat16
    )
    matrix = matrix.reshape(groups, values.shape[0], BLOCK, BLOCK).transpose(0, 2, 1, 3)
    return matrix.reshape(groups * BLOCK, values.shape[0] * BLOCK)


def swish_gate(summed, ff_local):
    return (jax.nn.silu(summed[:, :ff_local]) * summed[:, ff_local:]).astype(jnp.bfloat16)


def per_device(
    tokens,
    gate_vals,
    gate_scales,
    gate_rows,
    up_vals,
    up_scales,
    up_rows,
    down_vals,
    down_scales,
    down_rows,
):
    group_size = tokens.shape[1] // BLOCK
    row_offset = lax.axis_index("row") * group_size
    w_gate = dense_panel(gate_vals, gate_scales, gate_rows, row_offset, group_size)
    w_up = dense_panel(up_vals, up_scales, up_rows, row_offset, group_size)
    joined = jnp.concatenate([w_gate, w_up], axis=1)
    ff_local = w_gate.shape[1]
    ff_groups = ff_local // BLOCK
    w_down = dense_panel(
        down_vals, down_scales, down_rows, lax.axis_index("col") * ff_groups, ff_groups
    )
    gathered = lax.all_gather(tokens, "col", axis=0, tiled=True)
    selected = gathered
    summed = lax.psum_scatter(
        jnp.dot(selected, joined, preferred_element_type=jnp.float32).astype(jnp.bfloat16),
        "row",
        scatter_dimension=0,
        tiled=True,
    ).astype(jnp.float32)
    hidden_part = swish_gate(summed, ff_local)
    hidden = lax.all_gather(hidden_part, "row", axis=0, tiled=True)
    selected = hidden
    return lax.psum_scatter(
        jnp.dot(selected, w_down, preferred_element_type=jnp.float32).astype(jnp.bfloat16),
        "col",
        scatter_dimension=0,
        tiled=True,
    )


def solution(mesh):
    placed = (
        P("col", "row"),
        P("col", "row", None),
        P("col", "row"),
        P("col", "row"),
        P("col", "row", None),
        P("col", "row"),
        P("col", "row"),
        P("row", "col", None),
        P("row", "col"),
        P("row", "col"),
    )
    return jax.shard_map(
        per_device, mesh=mesh, in_specs=placed, out_specs=P("col", "row"), check_vma=False
    )
```

profile of v0, /device:TPU:8, one launch (start us, length us, event | category | flops | bytes accessed | tf_op | source)
XLA Modules:
  0.0 520.2 jit_solution(7833358821904089959)
XLA Ops:
  6.5 0.7 all-gather.3.cloned.1.call-update
  7.3 0.7 broadcast_subtract_fusion.1
  8.0 0.1 copy.28
  8.1 0.8 copy.27
  8.9 2.4 fusion.2
  11.3 4.9 reshape.27
  16.2 6.2 %copy.29 = bf16[8,28,64,64]{2,0,3,1:T(8,128)(2,1)} copy(bf16[8,28,64,64]{3,2,0,1:T(8,128)(2,1)} %reshape.27) | data formatting | bytes 3670016 | tf_op jit(solution)/shard_map/reshape | solution.py:17
  22.4 5.1 reshape.28
  27.5 0.1 copy.31
  27.6 0.1 copy.30
  27.7 2.5 fusion.3
  30.2 6.3 %reshape.29 = bf16[8,28,64,64]{3,2,0,1:T(8,128)(2,1)} reshape(bf16[8,28,4096]{2,0,1:T(8,128)(2,1)} %fusion.3) | data formatting | bytes 3670016 | tf_op jit(solution)/shard_map/reshape | solution.py:17
  36.6 6.2 %copy.32 = bf16[8,28,64,64]{2,0,3,1:T(8,128)(2,1)} copy(bf16[8,28,64,64]{3,2,0,1:T(8,128)(2,1)} %reshape.29) | data formatting | bytes 3670016 | tf_op jit(solution)/shard_map/reshape | solution.py:17
  42.8 5.9 %reshape.30 = bf16[512,1792]{0,1:T(8,128)(2,1)} reshape(bf16[8,64,28,64]{1,0,3,2:T(8,128)(2,1)} %bitcast.30) | data formatting | bytes 3670016 | tf_op jit(solution)/shard_map/reshape | solution.py:18
  48.7 46.1 %all-gather.3.cloned.1.call-done = bf16[2048,512]{1,0:T(8,128)(2,1)} async-done(((bf16[128,512]{1,0:T(8,128)(2,1)}), bf16[2048,512]{1,0:T(8,128)(2,1)}) %all-gather.3.cloned.1.call-update) | async-done | bytes 2097168 | tf_op jit(solution)/shard_map/all_gather | solution.py:47
  94.8 12.9 %fusion = bf16[2048,3584]{0,1:T(8,128)(2,1)} fusion(bf16[2048,512]{1,0:T(8,128)(2,1)} %all-gather.3.cloned.1.call-done, bf16[512,1792]{0,1:T(8,128)(2,1)} %reshape.30, bf16[512,1792]{0,1:T(8,128)(2,1)S(1)} %reshape.28), kind=kOutput, calls=%fused_computation.1 | convolution fusion | flops 7530872832 | bytes 20447232 | tf_op jit(solution)/shard_map/dot_general | solution.py:50
  107.6 18.7 %copy.37 = bf16[2048,3584]{1,0:T(8,128)(2,1)} copy(bf16[2048,3584]{0,1:T(8,128)(2,1)} %fusion) | data formatting | bytes 29360128
  126.4 191.3 %reduce-scatter.7.cloned.1.call-done = bf16[128,3584]{1,0:T(8,128)(2,1)} async-done(((bf16[2048,3584]{1,0:T(8,128)(2,1)}), bf16[128,3584]{1,0:T(8,128)(2,1)}) %reduce-scatter.7.cloned.1.call-update) | async-done | bytes 917520
  317.8 1.5 copy.38
  319.4 0.1 convert_element_type.64
  319.5 1.0 fusion.8
  320.6 0.2 reduce-scatter.5.cloned.1.call-start
  320.8 0.1 copy.33
  320.9 0.2 multiply_convert_fusion
  321.1 1.3 fusion.1
  322.5 1.0 copy.35
  323.5 5.0 reshape.31
  328.4 7.5 %copy.36 = bf16[28,64,8,64]{3,2,1,0:T(8,128)(2,1)} copy(bf16[28,64,8,64]{3,1,2,0:T(8,128)(2,1)} %bitcast.31) | data formatting | bytes 3670016 | tf_op jit(solution)/shard_map/transpose | solution.py:17
  336.0 5.0 reshape.32
  341.0 79.6 %all-gather.5.cloned.1.call-done = bf16[2048,1792]{0,1:T(8,128)(2,1)} async-done(((bf16[128,1792]{0,1:T(8,128)(2,1)}), bf16[2048,1792]{0,1:T(8,128)(2,1)}) %all-gather.5.cloned.1.call-update) | async-done | bytes 7340048 | tf_op jit(solution)/shard_map/all_gather | solution.py:56
  420.6 8.5 %convolution_convert_fusion.4 = bf16[2048,512]{1,0:T(8,128)(2,1)} fusion(bf16[2048,1792]{0,1:T(8,128)(2,1)} %all-gather.5.cloned.1.call-done, bf16[1792,512]{1,0:T(8,128)(2,1)S(1)} %reshape.32), kind=kOutput, calls=%fused_computation.11 | convolution fusion | flops 3759144960 | bytes 11272192 | tf_op jit(solution)/shard_map/dot_general | solution.py:59
  429.1 84.5 %reduce-scatter.5.cloned.1.call-done = bf16[128,512]{1,0:T(8,128)(2,1)} async-done(((bf16[2048,512]{1,0:T(8,128)(2,1)}), bf16[128,512]{1,0:T(8,128)(2,1)}) %reduce-scatter.5.cloned.1.call-update) | async-done | bytes 131088 | tf_op jit(solution)/shard_map/reduce_scatter | solution.py:58
  (17 shorter events, 0.2 us)
Async XLA Ops:
  6.5 88.2 %all-gather.3.cloned.1.call-start = ((), (), s32[]{:S(2)}) async-start(), calls=%async_computation.2 | async-start | bytes 2228224 | tf_op jit(solution)/shard_map/all_gather | solution.py:47
  7.3 310.5 %reduce-scatter.7.cloned.1.call-start = ((), (), s32[]{:S(2)}) async-start(), calls=%async_computation.5 | async-start | bytes 15597568
  22.4 5.2 %copy-start.3 = (f32[28,4]{0,1:T(4,128)S(1)}, f32[28,4]{0,1:T(4,128)}, u32[]{:S(2)}) copy-start(f32[28,4]{0,1:T(4,128)} %param.15) | copy-start | bytes 1348
  22.4 5.3 %copy-start.4 = (bf16[28,4,4096]{2,1,0:T(4,128)(2,1)S(1)}, bf16[28,4,4096]{2,1,0:T(4,128)(2,1)}, u32[]{:S(2)}) copy-start(bf16[28,4,4096]{2,1,0:T(4,128)(2,1)} %param.14) | copy-start | bytes 2752516
  126.4 294.2 %all-gather.5.cloned.1.call-start = ((), (), s32[]{:S(2)}) async-start(), calls=%async_computation.3 | async-start | bytes 7798784 | tf_op jit(solution)/shard_map/all_gather | solution.py:56
  319.3 1.5 copy-start.1
  319.4 1.5 copy-start.2
  319.4 1.5 copy-start
  320.6 193.1 %reduce-scatter.5.cloned.1.call-start = ((), (), s32[]{:S(2)}) async-start(), calls=%async_computation.4 | async-start | bytes 2228224 | tf_op jit(solution)/shard_map/reduce_scatter | solution.py:58
Sparse Core Ops, SparseCore 0:
  9.1 85.6 all-gather.2
  126.5 191.2 reduce-scatter.6
  320.7 99.8 all-gather.4
  429.3 84.3 reduce-scatter.4
where the time goes:
time: 522 us; the launch traced here: 520 us
  waiting for transfers between devices  402 us (77%)
  local copies, waits for them, and re-layouts  74.7 us (14%)
  matrix products  27.6 us (5%)
  between operations  13.2 us (3%)
    unnamed x5, waiting for transfers between devices  192 us
    reduce_scatter x1, waiting for transfers between devices, per_device(): lax.psum_scatter(jnp.dot(selected, w_down, preferred_element_type=jnp.flo...  84.5 us
    all_gather x1, waiting for transfers between devices, per_device(): hidden = lax.all_gather(hidden_part, 'row', axis=0, tiled=True)  79.6 us
    all_gather x1, waiting for transfers between devices, per_device(): gathered = lax.all_gather(tokens, 'col', axis=0, tiled=True)  46.1 us
    reshape x5, local copies, waits for them, and re-layouts, dense_panel(): matrix.reshape(groups, values.shape[0], BLOCK, BLOCK).transpose(0, 2, 1, 3)  28.6 us
    unnamed x15, local copies, waits for them, and re-layouts  21.3 us
    reshape x3, local copies, waits for them, and re-layouts, dense_panel(): return matrix.reshape(groups * BLOCK, values.shape[0] * BLOCK)  16 us
    dot_general x1, matrix products, per_device(): jnp.dot(selected, joined, preferred_element_type=jnp.float32)  12.9 us
  transfers between devices with their start and end apart: 4, of which 4 were waited for; matrix products, arithmetic and copies ran while one was open for 12% of the time, Pallas kernels for 0%

commit v1 on v0

v1 whole, which is shorter than its diff:
```python
import jax
import jax.numpy as jnp
from jax import lax
from jax.experimental import pallas as pl
from jax.experimental.pallas import tpu as pltpu
from jax.sharding import PartitionSpec as P

BF = jnp.bfloat16
F32 = jnp.float32
MESH = pl.DeviceIdType.MESH
NCH = 7
PIECES = ((0, 512, 8), (512, 256, 4), (768, 128, 2))


def mult(v, m):
    return pl.multiple_of(v, m)


def order_matrix(width, members):
    src = lax.broadcasted_iota(jnp.int32, (width, width), 0)
    k = lax.broadcasted_iota(jnp.int32, (width, width), 1)
    rl = lax.rem(k, members)
    hi = lax.div(k, members)
    i = lax.rem(hi, 32)
    h = lax.div(hi, 32)
    return jnp.where(src == rl * 64 + 2 * i + h, 1.0, 0.0).astype(BF)


def kernel(
    tok, comb, draw, tabs, tabd, out,
    x_all, tst, p512, wr, tb, dr, td, panel,
    own, bsend, brecv, own2, zsend, zrecv, hn, hid, wd, acc,
    o1s, o1r, o2s, o2r, own3, o3s,
    sem_t, sem_tx, sem_ws, sem_wr, sem_d, sem_b, sem_z, sem_hs, sem_hr, sem_o1, sem_o2, sem_o3,
):
    row = lax.axis_index("row")
    col = lax.axis_index("col")
    core = lax.rem(row, 2)
    y = lax.rem(lax.div(row, 2), 4)
    zh = lax.div(row, 8)
    x = lax.rem(col, 4)
    zl = lax.div(col, 4)
    b = lax.div(y, 2)
    kp = lax.rem(y, 2)
    a = lax.rem(lax.div(y + 1, 2), 2)
    g = core * 2 + kp
    sib = (row + 1 - 2 * core, col)
    row_a = row + 2 - 4 * kp
    dev_a = (row_a, col)
    dev_aa = (row_a + 1 - 2 * core, col)
    dev_b = (zh * 8 + (3 - y) * 2 + core, col)
    dev_z = ((1 - zh) * 8 + y * 2 + core, col)

    def xdev(d):
        return (row, zl * 4 + lax.rem(x + d, 4))

    def zdev(d):
        return (row, lax.rem(zl + d, 4) * 4 + x)

    def remote(src, dst, ss, rs, dev):
        return pltpu.make_async_remote_copy(
            src_ref=src, dst_ref=dst, send_sem=ss, recv_sem=rs, device_id=dev, device_id_type=MESH
        )

    def arrived(ref, sem):
        pltpu.make_async_copy(ref, ref, sem).wait()

    barrier = pltpu.get_barrier_semaphore()
    partners = [sib, dev_a, dev_aa, dev_b, dev_z] + [xdev(d) for d in (1, 2, 3)] + [zdev(d) for d in (1, 2, 3)]
    for dev in partners:
        pl.semaphore_signal(barrier, inc=1, device_id=dev, device_id_type=MESH)

    p512[...] = order_matrix(512, 8)
    tst[...] = jnp.dot(tok[...], p512[...], preferred_element_type=F32).astype(BF)
    myrow = mult((x * 4 + zl) * 64, 64)
    mylane = mult(core * 1024 + kp * 512, 512)
    corelane = mult(core * 1024, 1024)
    x_all[pl.ds(myrow, 64), pl.ds(mylane, 512)] = tst[pl.ds(mult(a * 64, 64), 64), :]

    pl.semaphore_wait(barrier, len(partners))

    sends = []

    def go(copy):
        copy.start()
        sends.append(copy)

    go(remote(tst.at[pl.ds(mult((1 - a) * 64, 64), 64), :],
              x_all.at[pl.ds(myrow, 64), pl.ds(mylane, 512)], sem_t.at[0, 0], sem_t.at[1, 0], dev_a))
    wdests = ((dev_a, core), (dev_aa, 1 - core), (sib, 1 - core))
    for n, (dev, half) in enumerate(wdests):
        go(remote(tabs.at[half], tb.at[g], sem_ws.at[8, n], sem_wr.at[8, g], dev))
    pltpu.make_async_copy(tabs.at[core], tb.at[g], sem_wr.at[8, g]).start()
    for p in range(NCH):
        for n, (dev, half) in enumerate(wdests):
            go(remote(comb.at[half * NCH + p], wr.at[p, g], sem_ws.at[p, n], sem_wr.at[p, g], dev))
        pltpu.make_async_copy(comb.at[core * NCH + p], wr.at[p, g], sem_wr.at[p, g]).start()
    go(remote(tabd, td.at[kp], sem_d.at[0, 0], sem_d.at[2, kp], dev_a))
    pltpu.make_async_copy(tabd, td.at[kp], sem_d.at[2, kp]).start()
    go(remote(draw, dr.at[kp], sem_d.at[0, 1], sem_d.at[1, kp], dev_a))
    pltpu.make_async_copy(draw, dr.at[kp], sem_d.at[1, kp]).start()

    def block(xs, zs):
        return x_all.at[pl.ds(mult((xs * 4 + zs) * 64, 64), 64), pl.ds(corelane, 1024)]

    def quarter(xs):
        return x_all.at[pl.ds(mult(xs * 256, 256), 256), pl.ds(corelane, 1024)]

    other = mult(core * 1024 + (1 - kp) * 512, 512)
    arrived(x_all.at[pl.ds(myrow, 64), pl.ds(other, 512)], sem_t.at[1, 0])
    for d in (1, 2, 3):
        go(remote(block(x, zl), block(x, zl), sem_t.at[0, d], sem_t.at[1, d], zdev(d)))
    for d in (2, 1, 3):
        go(remote(block(x, zl), block(x, zl), sem_tx.at[0, d, 0], sem_tx.at[1, d, 0], xdev(d)))
    for dz in (1, 3, 2):
        zs = lax.rem(zl + 4 - dz, 4)
        arrived(block(x, zs), sem_t.at[1, dz])
        for d in (2, 1, 3):
            go(remote(block(x, zs), block(x, zs), sem_tx.at[0, d, dz], sem_tx.at[1, d, dz], xdev(d)))
    go(remote(quarter(x), quarter(x), sem_tx.at[0, 0, 0], sem_tx.at[1, 0, 0], sib))

    lane = lax.broadcasted_iota(jnp.int32, (8, 128), 1)
    low = lane < 64
    sub = lax.broadcasted_iota(jnp.int32, (8, 128), 0)

    def pair(u0, u1, count):
        ev, od = [], []
        for i in range(count):
            v0 = u0[:, i * 128:(i + 1) * 128]
            v1 = u1[:, i * 128:(i + 1) * 128]
            ev.append(jnp.where(low, v0, pltpu.roll(v1, 64, 1)))
            od.append(jnp.where(low, pltpu.roll(v0, 64, 1), v1))
        return ev, od

    for q in range(4):
        arrived(tb.at[q], sem_wr.at[8, q])

    def build(p):
        for q in range(4):
            arrived(wr.at[p, q], sem_wr.at[p, q])
        code = tb[0, pl.ds(p, 1), :] + tb[1, pl.ds(p, 1), :] + tb[2, pl.ds(p, 1), :] + tb[3, pl.ds(p, 1), :]
        scale = tb[0, pl.ds(8 + p, 1), :] + tb[1, pl.ds(8 + p, 1), :] + tb[2, pl.ds(8 + p, 1), :] + tb[3, pl.ds(8 + p, 1), :]
        m = lax.broadcasted_iota(jnp.int32, (128, 128), 0).astype(F32)
        l = lax.broadcasted_iota(jnp.int32, (128, 128), 1)
        hit = jnp.logical_and(m == code, l < 64)
        factor = jnp.sum(jnp.where(hit, scale, 0.0), axis=1, keepdims=True)
        pick = jnp.where(hit, 1.0, 0.0).astype(BF)[:, :64]

        @pl.loop(0, 8)
        def _(n):
            lanes = pl.ds(mult(n * 512, 512), 512)
            slab = wr[p, :, :, lanes].reshape(64, 512)
            dense = jnp.dot(pick, slab, preferred_element_type=F32) * factor
            for q in range(4):
                for mat in range(2):
                    base = (q * 2 + mat) * 16
                    ev, od = pair(dense[base:base + 8], dense[base + 8:base + 16], 4)
                    for h, parts in ((0, ev), (1, od)):
                        panel[p, pl.ds(mult(q * 512 + h * 256 + n * 32, 32), 32), mat * 128:(mat + 1) * 128] = (
                            jnp.concatenate(parts, axis=0).astype(BF)
                        )

    EARLY = 3

    @pl.loop(0, EARLY)
    def _(p):
        build(p)

    for d in (1, 3, 2):
        xs = lax.rem(x + 4 - d, 4)
        for dz in range(4):
            arrived(block(xs, lax.rem(zl + 4 - dz, 4)), sem_tx.at[1, d, dz])
        go(remote(quarter(xs), quarter(xs), sem_tx.at[0, 0, d], sem_tx.at[1, 0, d], sib))
    siblane = mult((1 - core) * 1024, 1024)
    for d in (0, 1, 3, 2):
        xs = lax.rem(x + 4 - d, 4)
        arrived(x_all.at[pl.ds(mult(xs * 256, 256), 256), pl.ds(siblane, 1024)], sem_tx.at[1, 0, d])

    def product(p):
        def tokens_quarter(q):
            return jnp.dot(x_all[pl.ds(mult(q * 256, 256), 256), :], panel[p], preferred_element_type=F32)

        @pl.loop(0, 2)
        def _(i):
            bsend[p, pl.ds(mult(i * 256, 256), 256), :] = tokens_quarter(2 * (1 - b) + i).astype(BF)

        copy_b(p).start()

        @pl.loop(0, 2)
        def _(i):
            own[p, pl.ds(mult(i * 256, 256), 256), :] = tokens_quarter(2 * b + i)

    def copy_b(p):
        return remote(bsend.at[p], brecv.at[p], sem_b.at[0, p], sem_b.at[1, p], dev_b)

    def copy_z(p):
        return remote(zsend.at[p], zrecv.at[p], sem_z.at[0, p], sem_z.at[1, p], dev_z)

    def add_b(p):
        copy_b(p).wait_recv()
        away = pl.ds(mult((1 - zh) * 256, 256), 256)
        zsend[p] = (own[p, away, :] + brecv[p, away, :].astype(F32)).astype(BF)
        copy_z(p).start()
        keep = pl.ds(mult(zh * 256, 256), 256)
        own2[p] = own[p, keep, :] + brecv[p, keep, :].astype(F32)

    def add_z(p):
        copy_z(p).wait_recv()
        total = own2[p] + zrecv[p].astype(F32)
        gate = total[:, :128]
        hn[p] = (gate / (1.0 + jnp.exp(-gate)) * total[:, 128:]).astype(BF)

    def hpiece(s, c, q):
        off, width, _ = PIECES[s]
        return hid.at[pl.ds(mult(q * 256, 256), 256), pl.ds(mult(c * 896 + off, 128), width)]

    q_me = 2 * b + zh
    q_z = 2 * b + 1 - zh
    q_b = 2 * (1 - b) + zh
    q_bz = 2 * (1 - b) + 1 - zh

    def hcopy(s, n, q, dev):
        return remote(hpiece(s, core, q), hpiece(s, core, q), sem_hs.at[s, n], sem_hr.at[s, core * 4 + q], dev)

    def hstep_a(s):
        off, width, members = PIECES[s]
        first = (0, 4, 6)[s]
        parts = [hn[first + k] for k in range(width // 128)]
        nat = jnp.concatenate(parts, axis=1) if len(parts) > 1 else parts[0]
        order = p512[...] if s == 0 else order_matrix(width, members)
        hid[pl.ds(mult(q_me * 256, 256), 256), pl.ds(mult(core * 896 + off, 128), width)] = jnp.dot(
            nat, order, preferred_element_type=F32
        ).astype(BF)
        hcopy(s, 0, q_me, dev_z).start()
        hcopy(s, 1, q_me, dev_b).start()
        hcopy(s, 2, q_me, sib).start()

    def hstep_b(s):
        arrived(hpiece(s, core, q_z), sem_hr.at[s, core * 4 + q_z])
        hcopy(s, 3, q_z, dev_b).start()
        hcopy(s, 4, q_z, sib).start()

    def hstep_c(s):
        arrived(hpiece(s, core, q_b), sem_hr.at[s, core * 4 + q_b])
        hcopy(s, 5, q_b, sib).start()
        arrived(hpiece(s, core, q_bz), sem_hr.at[s, core * 4 + q_bz])
        hcopy(s, 6, q_bz, sib).start()

    def hstep_d(s):
        for q in range(4):
            arrived(hpiece(s, 1 - core, q), sem_hr.at[s, (1 - core) * 4 + q])

    def build_down():
        for side in range(2):
            arrived(td.at[side], sem_d.at[2, side])
            arrived(dr.at[side], sem_d.at[1, side])

        @pl.loop(0, 2)
        def _(side):
            code = td[side, 0:1, :]
            scale = td[side, 1:2, :]
            m = lax.broadcasted_iota(jnp.int32, (384, 128), 0)
            within = lax.rem(m, 8)
            piece = lax.rem(lax.div(m, 64), 3)
            members = jnp.where(piece == 0, 8, jnp.where(piece == 1, 4, 2))
            mm = (m - within + lax.rem(within, members)).astype(F32)
            hit = mm == code
            factor = jnp.sum(jnp.where(hit, scale, 0.0), axis=1, keepdims=True)
            pick = jnp.where(hit, 1.0, 0.0).astype(BF)[:, :112]

            @pl.loop(0, 4)
            def _(n):
                lanes = pl.ds(mult(n * 1024, 1024), 1024)
                dense = jnp.dot(pick, dr[side, :, lanes], preferred_element_type=F32) * factor
                for cc in range(2):
                    for s, (off, width, count) in enumerate(PIECES):
                        dup = 8 // count
                        for jp in range(4):
                            base = ((cc * 3 + s) * 8 + 2 * jp) * 8

                            def merged(r0):
                                u = dense[r0:r0 + 8]
                                tiles = [u[:, i * 128:(i + 1) * 128] for i in range(8)]
                                while len(tiles) > 8 // dup:
                                    half = 4 if len(tiles) == 8 and dup == 2 else None
                                    tiles = merge(tiles, dup)
                                return jnp.concatenate(tiles, axis=1)

                            def merge(tiles, dup):
                                res = []
                                for k in range(len(tiles) // dup):
                                    t = tiles[k * dup]
                                    for e in range(1, dup):
                                        t = jnp.where(lax.div(sub, count) == e, tiles[k * dup + e], t)
                                    res.append(t)
                                return res

                            ev, od = pair(merged(base), merged(base + 8), 8 // dup)
                            rows = 8 * count
                            for h, parts in ((0, ev), (1, od)):
                                start = mult(cc * 896 + off + h * (width // 2) + n * rows, 16)
                                wd[pl.ds(start, rows), pl.ds(mult(side * 512 + jp * 128, 128), 128)] = (
                                    jnp.concatenate(parts, axis=0) if len(parts) > 1 else parts[0]
                                ).astype(BF)

    @pl.loop(0, NCH + 3)
    def _(p):
        @pl.when(p < NCH)
        def _():
            @pl.when(p >= EARLY)
            def _():
                build(p)

            product(p)

        @pl.when(p == 7)
        def _():
            build_down()

        @pl.when(jnp.logical_and(p >= 1, p <= NCH))
        def _():
            add_b(p - 1)

        @pl.when(p >= 3)
        def _():
            add_z(p - 3)

        @pl.when(p == 6)
        def _():
            hstep_a(0)

        @pl.when(p == 8)
        def _():
            hstep_a(1)
            hstep_b(0)

        @pl.when(p == 9)
        def _():
            hstep_a(2)

    hstep_c(0)
    hstep_b(1)
    hstep_b(2)
    hstep_d(0)

    @pl.loop(0, 4)
    def _(q):
        rows = pl.ds(mult(q * 256, 256), 256)
        for n in range(2):
            cols = slice(n * 512, (n + 1) * 512)
            acc[rows, cols] = jnp.dot(hid[rows, 0:512], wd[0:512, cols], preferred_element_type=F32) + jnp.dot(
                hid[rows, 896:1408], wd[896:1408, cols], preferred_element_type=F32
            )

    for s in (1, 2):
        hstep_c(s)
    for s in (1, 2):
        hstep_d(s)

    def final(q, n):
        rows = pl.ds(mult(q * 256, 256), 256)
        cols = pl.ds(mult(n * 512, 512), 512)
        return (
            acc[rows, cols]
            + jnp.dot(hid[rows, 512:896], wd[512:896, cols], preferred_element_type=F32)
            + jnp.dot(hid[rows, 1408:1792], wd[1408:1792, cols], preferred_element_type=F32)
        )

    def copy_o1(i, d):
        return remote(o1s.at[i, d - 1], o1r.at[i, d - 1], sem_o1.at[0, i, d - 1], sem_o1.at[1, i, d - 1], xdev(d))

    def copy_o2(i, d):
        return remote(o2s.at[i, d - 1], o2r.at[i, d - 1], sem_o2.at[0, i, d - 1], sem_o2.at[1, i, d - 1], zdev(d))

    for i in range(2):
        n = 1 - kp if i == 0 else kp
        for d in (2, 1, 3):
            o1s[i, d - 1] = final(lax.rem(x + d, 4), n).astype(BF)
            copy_o1(i, d).start()
    mine = pl.ds(mult(x * 256, 256), 256)
    for i in range(2):
        n = 1 - kp if i == 0 else kp
        acc[mine, pl.ds(mult(n * 512, 512), 512)] = final(x, n)

    for i in range(2):
        n = 1 - kp if i == 0 else kp
        for d in (1, 3, 2):
            copy_o1(i, d).wait_recv()

        def summed(zs):
            r = pl.ds(mult(zs * 64, 64), 64)
            total = acc[pl.ds(mult(x * 256 + zs * 64, 64), 64), pl.ds(mult(n * 512, 512), 512)]
            for d in range(3):
                total = total + o1r[i, d, r, :].astype(F32)
            return total

        for d in (1, 3, 2):
            o2s[i, d - 1] = summed(lax.rem(zl + d, 4)).astype(BF)
            copy_o2(i, d).start()
        own3[i] = summed(zl)

    o3 = remote(o3s, out.at[pl.ds(mult(a * 64, 64), 64), :], sem_o3.at[0], sem_o3.at[1], dev_a)
    for i in range(2):
        for d in (1, 3, 2):
            copy_o2(i, d).wait_recv()
        total = own3[i]
        for d in range(3):
            total = total + o2r[i, d].astype(F32)
        if i == 0:
            o3s[...] = total.astype(BF)
            o3.start()
        else:
            out[pl.ds(mult(a * 64, 64), 64), :] = total.astype(BF)

    for copy in sends:
        copy.wait_send()

    @pl.loop(0, NCH)
    def _(p):
        copy_b(p).wait_send()
        copy_z(p).wait_send()

    for s in range(3):
        for n, q in ((0, q_me), (1, q_me), (2, q_me), (3, q_z), (4, q_z), (5, q_b), (6, q_bz)):
            hcopy(s, n, q, sib).wait_send()
    for i in range(2):
        for d in (1, 2, 3):
            copy_o1(i, d).wait_send()
            copy_o2(i, d).wait_send()
    o3.wait_send()
    arrived(out.at[pl.ds(mult((1 - a) * 64, 64), 64), :], sem_o3.at[1])


def per_device(
    tokens, gate_vals, gate_scales, gate_rows, up_vals, up_scales, up_rows, down_vals, down_scales, down_rows
):
    row = lax.axis_index("row")
    col = lax.axis_index("col")
    g = (row % 2) * 2 + (row // 2) % 2
    comb = jnp.concatenate([gate_vals.reshape(14, 8, 4096), up_vals.reshape(14, 8, 4096)], axis=1)
    draw = down_vals.transpose(1, 0, 2).reshape(112, 4096)

    lane = jnp.arange(128, dtype=jnp.int32)

    def chunked(gate, up):
        both = jnp.stack([gate.reshape(2, 7, 8), up.reshape(2, 7, 8)], axis=2).reshape(2, 7, 16)
        return jnp.pad(jnp.tile(both, (1, 1, 8)), ((0, 0), (0, 1), (0, 0)))

    where = chunked(gate_rows - row * 8, up_rows - row * 8) + 8 * (lane // 4)
    tabs = jnp.concatenate([where.astype(F32), chunked(gate_scales, up_scales)], axis=1)
    tabs = jnp.where(lane // 16 == g, tabs, 0.0)

    rel = down_rows - col * 28
    cc = rel // 14
    rr = rel - cc * 14
    piece = (rr >= 8).astype(jnp.int32) + (rr >= 12).astype(jnp.int32)
    rl = rr - jnp.where(piece == 0, 0, jnp.where(piece == 1, 8, 12))
    code = ((cc * 3 + piece) * 8 + jnp.arange(8, dtype=jnp.int32)[:, None]) * 8 + rl
    code = jnp.pad(code.T.reshape(1, 112).astype(F32), ((0, 0), (0, 16)), constant_values=-1.0)
    tabd = jnp.concatenate(
        [code, jnp.pad(down_scales.T.reshape(1, 112), ((0, 0), (0, 16))), jnp.zeros((6, 128), F32)], axis=0
    )

    vm = pl.BlockSpec(memory_space=pltpu.VMEM)
    hb = pl.BlockSpec(memory_space=pl.ANY)
    dma = pltpu.SemaphoreType.DMA
    return pl.pallas_call(
        kernel,
        out_shape=jax.ShapeDtypeStruct((128, 512), BF),
        in_specs=[vm, hb, hb, vm, vm],
        out_specs=vm,
        scratch_shapes=[
            pltpu.VMEM((1024, 2048), BF),
            pltpu.VMEM((128, 512), BF),
            pltpu.VMEM((512, 512), BF),
            pltpu.VMEM((NCH, 4, 16, 4096), BF),
            pltpu.VMEM((4, 16, 128), F32),
            pltpu.VMEM((2, 112, 4096), BF),
            pltpu.VMEM((2, 8, 128), F32),
            pltpu.VMEM((NCH, 2048, 256), BF),
            pltpu.VMEM((NCH, 512, 256), F32),
            pltpu.VMEM((NCH, 512, 256), BF),
            pltpu.VMEM((NCH, 512, 256), BF),
            pltpu.VMEM((NCH, 256, 256), F32),
            pltpu.VMEM((NCH, 256, 256), BF),
            pltpu.VMEM((NCH, 256, 256), BF),
            pltpu.VMEM((NCH, 256, 128), BF),
            pltpu.VMEM((1024, 1792), BF),
            pltpu.VMEM((1792, 1024), BF),
            pltpu.VMEM((1024, 1024), F32),
            pltpu.VMEM((2, 3, 256, 512), BF),
            pltpu.VMEM((2, 3, 256, 512), BF),
            pltpu.VMEM((2, 3, 64, 512), BF),
            pltpu.VMEM((2, 3, 64, 512), BF),
            pltpu.VMEM((2, 64, 512), F32),
            pltpu.VMEM((64, 512), BF),
            dma((2, 4)),
            dma((2, 4, 4)),
            dma((9, 3)),
            dma((9, 4)),
            dma((3, 2)),
            dma((2, NCH)),
            dma((2, NCH)),
            dma((3, 7)),
            dma((3, 8)),
            dma((2, 2, 3)),
            dma((2, 2, 3)),
            dma((2,)),
        ],
        compiler_params=pltpu.CompilerParams(
            collective_id=0, has_side_effects=True, vmem_limit_bytes=62 * 1024 * 1024
        ),
        name="gated_layer",
    )(tokens, comb, draw, tabs, tabd)


def solution(mesh):
    placed = (
        P("col", "row"),
        P("col", "row", None),
        P("col", "row"),
        P("col", "row"),
        P("col", "row", None),
        P("col", "row"),
        P("col", "row"),
        P("row", "col", None),
        P("row", "col"),
        P("row", "col"),
    )
    return jax.shard_map(
        per_device, mesh=mesh, in_specs=placed, out_specs=P("col", "row"), check_vma=False
    )
```

time: 522 us -> 159 us (0.30)
  waiting for transfers between devices: 402 us -> 0 us
  Pallas kernels: 0 us -> 151 us
  local copies, waits for them, and re-layouts: 74.7 us -> 5.04 us
  matrix products: 27.6 us -> 0 us
  between operations: 13.2 us -> 0.23 us
    unnamed x5 -> x0, waiting for transfers between devices: 192 us -> none
    pallas_call x0 -> x1, Pallas kernels: none -> 151 us  [per_device(): pl.pallas_call(kernel, out_shape=jax.ShapeDtypeStruct((128, 512), BF), in...]
    all_gather x2 -> x0, waiting for transfers between devices: 126 us -> none  [the longest x1 79.6 us: per_device(): hidden = lax.all_gather(hidden_part, 'row', axis=0, tiled=True)]
    reduce_scatter x1 -> x0, waiting for transfers between devices: 84.5 us -> none  [per_device(): lax.psum_scatter(jnp.dot(selected, w_down, preferred_element_type=jnp.flo...]
    reshape x8 -> x3, local copies, waits for them, and re-layouts: 44.6 us -> 2.01 us  [the longest x1 1.72 us: per_device(): up_vals.reshape(14, 8, 4096)]
    dot_general x5 -> x0, matrix products: 27.6 us -> none  [the longest x1 12.9 us: per_device(): jnp.dot(selected, joined, preferred_element_type=jnp.float32)]
    unnamed x15 -> x17, local copies, waits for them, and re-layouts: 21.3 us -> 1.81 us
    transpose x1, local copies, waits for them, and re-layouts: 7.55 us -> 0.08 us  [per_device(): down_scales.T.reshape(1, 112)]
  transfers between devices with their start and end apart: 4 -> 0, of which waited for: 4 -> 0; matrix products, arithmetic and copies ran while one was open for 12% -> 0% of each run, Pallas kernels for 0% -> 0%
where the time goes in v1:
time: 159 us
  Pallas kernels  151 us (95%)
  local copies, waits for them, and re-layouts  5.04 us (3%)
  other arithmetic  2.71 us (2%)
    pallas_call x1, Pallas kernels, per_device(): pl.pallas_call(kernel, out_shape=jax.ShapeDtypeStruct((128, 512), BF), in...  151 us

profile of v1, /device:TPU:8, one launch (start us, length us, event | category | flops | bytes accessed | tf_op | source)
XLA Modules:
  0.0 158.5 jit_solution(651480201712086149)
XLA Ops:
  0.0 1.7 %reshape.49 = bf16[14,8,4096]{2,1,0:T(8,128)(2,1)S(1)} reshape(bf16[28,4,4096]{2,1,0:T(4,128)(2,1)} %param.14) | data formatting | bytes 1835008 | tf_op jit(solution)/shard_map/reshape | solution.py:440
  1.7 0.0 copy-done
  1.7 0.2 reshape.48
  2.0 0.0 copy-start.3
  2.0 0.0 copy-start.4
  2.0 0.0 copy-start.5
  2.0 0.0 copy-start.6
  2.0 0.0 copy-start.1
  2.0 0.0 copy-start.2
  2.0 1.4 pad_maximum_fusion.comb
  3.4 0.0 copy-done.3
  3.4 0.1 copy.22
  3.5 0.1 stack_reshape.15
  3.6 0.1 copy.21
  3.7 0.1 stack_reshape.14
  3.8 0.1 tile.23
  3.9 0.1 tile.25
  4.0 0.1 copy.18
  4.1 0.1 stack_reshape.13
  4.2 0.1 copy.17
  4.3 0.1 stack_reshape.12
  4.4 0.1 tile.20
  4.5 0.1 tile.22
  4.6 0.6 fusion.tabs
  5.3 0.1 copy.26
  5.3 0.1 reshape.51
  5.5 0.1 copy.25
  5.6 0.1 convert_element_type.35
  5.7 0.1 pad.22.clone
  5.7 0.7 fusion.1.tabd
  6.4 150.6 %gated_layer.1 = bf16[128,512]{1,0:T(8,128)(2,1)} custom-call(bf16[128,512]{1,0:T(8,128)(2,1)} %tok.1, bf16[14,16,4096]{2,1,0:T(8,128)(2,1)} %pad_maximum_fusion.comb, bf16[112,4096]{1,0:T(8,128)(2,1)} %bitcast.18, f32[2,16,128]{2,1,0:T(8,128)} %fusion.tabs, f32[8,128]{1,0:T(8,128)} %fusion.1.tabd), custom_call_target="tpu_custom_call" | custom-call | tf_op jit(solution)/shard_map/gated_layer/pallas_call | solution.py:467
  157.0 1.6 copy.28
  (20 shorter events, 0.1 us)
Async XLA Ops:
  0.0 1.7 %copy-start = (bf16[28,4,4096]{2,1,0:T(4,128)(2,1)S(1)}, bf16[28,4,4096]{2,1,0:T(4,128)(2,1)}, u32[]{:S(2)}) copy-start(bf16[28,4,4096]{2,1,0:T(4,128)(2,1)} %param.11) | copy-start | bytes 2752516
  2.0 1.4 copy-start.3
  2.0 1.6 %copy-start.4 = (f32[28,4]{0,1:T(4,128)S(1)}, f32[28,4]{0,1:T(4,128)}, u32[]{:S(2)}) copy-start(f32[28,4]{0,1:T(4,128)} %param.12) | copy-start | bytes 1348
  2.0 2.0 %copy-start.5 = (s32[28,4]{0,1:T(4,128)S(1)}, s32[28,4]{0,1:T(4,128)}, u32[]{:S(2)}) copy-start(s32[28,4]{0,1:T(4,128)} %param.16) | copy-start | bytes 1348
  2.0 2.0 %copy-start.6 = (s32[28,4]{0,1:T(4,128)S(1)}, s32[28,4]{0,1:T(4,128)}, u32[]{:S(2)}) copy-start(s32[28,4]{0,1:T(4,128)} %param.13) | copy-start | bytes 1348
  2.0 3.3 %copy-start.1 = (f32[8,14]{1,0:T(8,128)S(1)}, f32[8,14]{1,0:T(8,128)}, u32[]{:S(2)}) copy-start(f32[8,14]{1,0:T(8,128)} %param.18) | copy-start | bytes 1348
  2.0 3.4 %copy-start.2 = (s32[8,14]{1,0:T(8,128)S(1)}, s32[8,14]{1,0:T(8,128)}, u32[]{:S(2)}) copy-start(s32[8,14]{1,0:T(8,128)} %param.19) | copy-start | bytes 1348

commit v2 on v1

--- a/solution.py
+++ b/solution.py
@@ -17,21 +17,19 @@
 
 
 def order_matrix(width, members):
+    shift = members.bit_length() - 1
+    k = lax.broadcasted_iota(jnp.int32, (1, width), 1)
+    source = ((k & (members - 1)) << 6) + (((k >> shift) & 31) << 1) + (k >> (shift + 5))
     src = lax.broadcasted_iota(jnp.int32, (width, width), 0)
-    k = lax.broadcasted_iota(jnp.int32, (width, width), 1)
-    rl = lax.rem(k, members)
-    hi = lax.div(k, members)
-    i = lax.rem(hi, 32)
-    h = lax.div(hi, 32)
-    return jnp.where(src == rl * 64 + 2 * i + h, 1.0, 0.0).astype(BF)
+    return jnp.where(src == source, 1.0, 0.0).astype(BF)
 
 
 def kernel(
-    tok, comb, draw, tabs, tabd, out,
-    x_all, tst, p512, wr, tb, dr, td, panel,
+    tok, graw, uraw, draw, grows, gscales, urows, uscales, drows, dscales, out,
+    raw, comb, tabs, tabd, x_all, tst, p512, wr, tb, dr, td, panel,
     own, bsend, brecv, own2, zsend, zrecv, hn, hid, wd, acc,
-    o1s, o1r, o2s, o2r, own3, o3s,
-    sem_t, sem_tx, sem_ws, sem_wr, sem_d, sem_b, sem_z, sem_hs, sem_hr, sem_o1, sem_o2, sem_o3,
+    fars, farr, nears, nearr, o2s, o2r, own3, o3s,
+    sem_raw, sem_t, sem_tx, sem_ws, sem_wr, sem_d, sem_b, sem_z, sem_hs, sem_hr, sem_far, sem_near, sem_o2, sem_o3,
 ):
     row = lax.axis_index("row")
     col = lax.axis_index("col")
@@ -65,6 +63,10 @@
     def arrived(ref, sem):
         pltpu.make_async_copy(ref, ref, sem).wait()
 
+    raw_copies = [pltpu.make_async_copy(src, raw.at[k], sem_raw.at[k]) for k, src in enumerate((graw, uraw))]
+    for copy in raw_copies:
+        copy.start()
+
     barrier = pltpu.get_barrier_semaphore()
     partners = [sib, dev_a, dev_aa, dev_b, dev_z] + [xdev(d) for d in (1, 2, 3)] + [zdev(d) for d in (1, 2, 3)]
     for dev in partners:
@@ -87,18 +89,70 @@
 
     go(remote(tst.at[pl.ds(mult((1 - a) * 64, 64), 64), :],
               x_all.at[pl.ds(myrow, 64), pl.ds(mylane, 512)], sem_t.at[0, 0], sem_t.at[1, 0], dev_a))
+    lane = lax.broadcasted_iota(jnp.int32, (8, 128), 1)
+    sub = lax.broadcasted_iota(jnp.int32, (8, 128), 0)
+    low = lane < 64
+
+    jlane = lax.broadcasted_iota(jnp.int32, (8, 28), 1)
+    jsub = lax.broadcasted_iota(jnp.int32, (8, 28), 0)
+    for half in range(2):
+        where = jnp.where((lane >> 4) == g, (lane >> 2) << 3, 0).astype(F32)
+        scales = jnp.zeros((8, 128), F32)
+        for mat, (rows_ref, scales_ref) in enumerate(((grows, gscales), (urows, uscales))):
+            rel = (rows_ref[...] - row * 8).astype(F32)
+            sc = scales_ref[...]
+            for jj in range(2):
+                mask = jlane == 14 * half + 2 * jsub + jj
+                for k in range(4):
+                    here = lane == 16 * g + 8 * mat + 4 * jj + k
+                    v = jnp.sum(jnp.where(mask, rel[k:k + 1], 0.0), axis=1, keepdims=True)
+                    w = jnp.sum(jnp.where(mask, sc[k:k + 1], 0.0), axis=1, keepdims=True)
+                    where = where + jnp.where(here, v, 0.0)
+                    scales = scales + jnp.where(here, w, 0.0)
+        tabs[half, 0:8, :] = where
+        tabs[half, 8:16, :] = scales
+    rel = drows[...] - col * 28
+    cc = jnp.where(rel >= 14, 1, 0)
+    rr = rel - 14 * cc
+    piece = jnp.where(rr >= 12, 2, jnp.where(rr >= 8, 1, 0))
+    rl = rr - jnp.where(rr >= 12, 12, jnp.where(rr >= 8, 8, 0))
+    j8 = lax.broadcasted_iota(jnp.int32, (8, 14), 0)
+    code = ((((cc * 3 + piece) * 8 + j8) << 3) + rl).astype(F32)
+    sc = dscales[...]
+    cspread = jnp.zeros((8, 128), F32)
+    sspread = jnp.zeros((8, 128), F32)
+    for k in range(14):
+        here = lane == 8 * k + sub
+        cspread = cspread + jnp.where(here, code[:, k:k + 1], 0.0)
+        sspread = sspread + jnp.where(here, sc[:, k:k + 1], 0.0)
+    tabd[...] = jnp.where(
+        sub == 0,
+        jnp.where(lane < 112, jnp.sum(cspread, axis=0, keepdims=True), -1.0),
+        jnp.sum(sspread, axis=0, keepdims=True),
+    )
+
     wdests = ((dev_a, core), (dev_aa, 1 - core), (sib, 1 - core))
-    for n, (dev, half) in enumerate(wdests):
-        go(remote(tabs.at[half], tb.at[g], sem_ws.at[8, n], sem_wr.at[8, g], dev))
-    pltpu.make_async_copy(tabs.at[core], tb.at[g], sem_wr.at[8, g]).start()
-    for p in range(NCH):
+
+    def send_weights():
         for n, (dev, half) in enumerate(wdests):
-            go(remote(comb.at[half * NCH + p], wr.at[p, g], sem_ws.at[p, n], sem_wr.at[p, g], dev))
-        pltpu.make_async_copy(comb.at[core * NCH + p], wr.at[p, g], sem_wr.at[p, g]).start()
-    go(remote(tabd, td.at[kp], sem_d.at[0, 0], sem_d.at[2, kp], dev_a))
-    pltpu.make_async_copy(tabd, td.at[kp], sem_d.at[2, kp]).start()
-    go(remote(draw, dr.at[kp], sem_d.at[0, 1], sem_d.at[1, kp], dev_a))
-    pltpu.make_async_copy(draw, dr.at[kp], sem_d.at[1, kp]).start()
+            go(remote(tabs.at[half], tb.at[g], sem_ws.at[8, n], sem_wr.at[8, g], dev))
+        pltpu.make_async_copy(tabs.at[core], tb.at[g], sem_wr.at[8, g]).start()
+        for copy in raw_copies:
+            copy.wait()
+
+        @pl.loop(0, NCH)
+        def _(p):
+            for half in range(2):
+                for k in range(2):
+                    comb[half * NCH + p, 8 * k:8 * k + 8, :] = raw[k, pl.ds(2 * (half * NCH + p), 2)].reshape(8, 4096)
+            for n, (dev, half) in enumerate(wdests):
+                remote(comb.at[half * NCH + p], wr.at[p, g], sem_ws.at[p, n], sem_wr.at[p, g], dev).start()
+            pltpu.make_async_copy(comb.at[core * NCH + p], wr.at[p, g], sem_wr.at[p, g]).start()
+
+        go(remote(tabd, td.at[kp], sem_d.at[0, 0], sem_d.at[2, kp], dev_a))
+        pltpu.make_async_copy(tabd, td.at[kp], sem_d.at[2, kp]).start()
+        go(remote(draw, dr.at[kp], sem_d.at[0, 1], sem_d.at[1, kp], dev_a))
+        pltpu.make_async_copy(draw, dr.at[kp], sem_d.at[1, kp]).start()
 
     def block(xs, zs):
         return x_all.at[pl.ds(mult((xs * 4 + zs) * 64, 64), 64), pl.ds(corelane, 1024)]
@@ -108,20 +162,32 @@
 
     other = mult(core * 1024 + (1 - kp) * 512, 512)
     arrived(x_all.at[pl.ds(myrow, 64), pl.ds(other, 512)], sem_t.at[1, 0])
-    for d in (1, 2, 3):
+    for d in (1, 3, 2):
         go(remote(block(x, zl), block(x, zl), sem_t.at[0, d], sem_t.at[1, d], zdev(d)))
-    for d in (2, 1, 3):
-        go(remote(block(x, zl), block(x, zl), sem_tx.at[0, d, 0], sem_tx.at[1, d, 0], xdev(d)))
-    for dz in (1, 3, 2):
+
+    def along_x(zs, dz):
+        for d in (1, 3):
+            go(remote(block(x, zs), block(x, zs), sem_tx.at[0, d, dz], sem_tx.at[1, d, dz], xdev(d)))
+
+    def from_z(dz):
         zs = lax.rem(zl + 4 - dz, 4)
         arrived(block(x, zs), sem_t.at[1, dz])
-        for d in (2, 1, 3):
-            go(remote(block(x, zs), block(x, zs), sem_tx.at[0, d, dz], sem_tx.at[1, d, dz], xdev(d)))
+        along_x(zs, dz)
+
+    def onward(dz):
+        d = 1 if dz % 2 == 0 else 3
+        source = block(lax.rem(x + 4 - d, 4), lax.rem(zl + 4 - dz, 4))
+        arrived(source, sem_tx.at[1, d, dz])
+        go(remote(source, source, sem_tx.at[0, 2, dz], sem_tx.at[1, 2, dz], xdev(d)))
+
+    along_x(zl, 0)
+    send_weights()
+    from_z(1)
+    onward(0)
+    from_z(3)
+    onward(1)
+    from_z(2)
     go(remote(quarter(x), quarter(x), sem_tx.at[0, 0, 0], sem_tx.at[1, 0, 0], sib))
-
-    lane = lax.broadcasted_iota(jnp.int32, (8, 128), 1)
-    low = lane < 64
-    sub = lax.broadcasted_iota(jnp.int32, (8, 128), 0)
 
     def pair(u0, u1, count):
         ev, od = [], []
@@ -161,14 +227,18 @@
                         )
 
     EARLY = 3
-
-    @pl.loop(0, EARLY)
+    build(0)
+    onward(3)
+    onward(2)
+
+    @pl.loop(1, EARLY)
     def _(p):
         build(p)
 
     for d in (1, 3, 2):
         xs = lax.rem(x + 4 - d, 4)
-        for dz in range(4):
+        waits = {1: (1, 3), 3: (0, 2), 2: (0, 1, 2, 3)}[d]
+        for dz in waits:
             arrived(block(xs, lax.rem(zl + 4 - dz, 4)), sem_tx.at[1, d, dz])
         go(remote(quarter(xs), quarter(xs), sem_tx.at[0, 0, d], sem_tx.at[1, 0, d], sib))
     siblane = mult((1 - core) * 1024, 1024)
@@ -180,27 +250,31 @@
         def tokens_quarter(q):
             return jnp.dot(x_all[pl.ds(mult(q * 256, 256), 256), :], panel[p], preferred_element_type=F32)
 
+        def send_quarter(i):
+            bsend[p, pl.ds(mult(i * 256, 256), 256), :] = tokens_quarter(2 * (1 - b) + i).astype(BF)
+            copy_b(p, i).start()
+
         @pl.loop(0, 2)
-        def _(i):
-            bsend[p, pl.ds(mult(i * 256, 256), 256), :] = tokens_quarter(2 * (1 - b) + i).astype(BF)
-
-        copy_b(p).start()
+        def _(k):
+            send_quarter(lax.rem(1 - zh + k, 2))
 
         @pl.loop(0, 2)
         def _(i):
             own[p, pl.ds(mult(i * 256, 256), 256), :] = tokens_quarter(2 * b + i)
 
-    def copy_b(p):
-        return remote(bsend.at[p], brecv.at[p], sem_b.at[0, p], sem_b.at[1, p], dev_b)
+    def copy_b(p, i):
+        rows = pl.ds(mult(i * 256, 256), 256)
+        return remote(bsend.at[p, rows, :], brecv.at[p, rows, :], sem_b.at[0, p, i], sem_b.at[1, p, i], dev_b)
 
     def copy_z(p):
         return remote(zsend.at[p], zrecv.at[p], sem_z.at[0, p], sem_z.at[1, p], dev_z)
 
     def add_b(p):
-        copy_b(p).wait_recv()
+        copy_b(p, 1 - zh).wait_recv()
         away = pl.ds(mult((1 - zh) * 256, 256), 256)
         zsend[p] = (own[p, away, :] + brecv[p, away, :].astype(F32)).astype(BF)
         copy_z(p).start()
+        copy_b(p, zh).wait_recv()
         keep = pl.ds(mult(zh * 256, 256), 256)
         own2[p] = own[p, keep, :] + brecv[p, keep, :].astype(F32)
 
@@ -260,10 +334,11 @@
             code = td[side, 0:1, :]
             scale = td[side, 1:2, :]
             m = lax.broadcasted_iota(jnp.int32, (384, 128), 0)
-            within = lax.rem(m, 8)
-            piece = lax.rem(lax.div(m, 64), 3)
-            members = jnp.where(piece == 0, 8, jnp.where(piece == 1, 4, 2))
-            mm = (m - within + lax.rem(within, members)).astype(F32)
+            within = m & 7
+            sixes = m >> 6
+            piece = jnp.where(sixes >= 3, sixes - 3, sixes)
+            last = jnp.where(piece == 0, 7, jnp.where(piece == 1, 3, 1))
+            mm = (m - within + (within & last)).astype(F32)
             hit = mm == code
             factor = jnp.sum(jnp.where(hit, scale, 0.0), axis=1, keepdims=True)
             pick = jnp.where(hit, 1.0, 0.0).astype(BF)[:, :112]
@@ -282,7 +357,6 @@
                                 u = dense[r0:r0 + 8]
                                 tiles = [u[:, i * 128:(i + 1) * 128] for i in range(8)]
                                 while len(tiles) > 8 // dup:
-                                    half = 4 if len(tiles) == 8 and dup == 2 else None
                                     tiles = merge(tiles, dup)
                                 return jnp.concatenate(tiles, axis=1)
 
@@ -291,7 +365,7 @@
                                 for k in range(len(tiles) // dup):
                                     t = tiles[k * dup]
                                     for e in range(1, dup):
-                                        t = jnp.where(lax.div(sub, count) == e, tiles[k * dup + e], t)
+                                        t = jnp.where((sub >> (count.bit_length() - 1)) == e, tiles[k * dup + e], t)
                                     res.append(t)
                                 return res
 
@@ -357,119 +431,122 @@
     for s in (1, 2):
         hstep_d(s)
 
-    def final(q, n):
+    def columns(i):
+        return mult((1 - kp if i < 2 else kp) * 512 + (i % 2) * 256, 256)
+
+    def final(q, i):
         rows = pl.ds(mult(q * 256, 256), 256)
-        cols = pl.ds(mult(n * 512, 512), 512)
+        cols = pl.ds(columns(i), 256)
         return (
             acc[rows, cols]
             + jnp.dot(hid[rows, 512:896], wd[512:896, cols], preferred_element_type=F32)
             + jnp.dot(hid[rows, 1408:1792], wd[1408:1792, cols], preferred_element_type=F32)
         )
 
-    def copy_o1(i, d):
-        return remote(o1s.at[i, d - 1], o1r.at[i, d - 1], sem_o1.at[0, i, d - 1], sem_o1.at[1, i, d - 1], xdev(d))
+    def copy_far(i):
+        return remote(fars.at[i], farr.at[i], sem_far.at[0, i], sem_far.at[1, i], xdev(1 if i % 2 == 0 else 3))
+
+    def copy_near(d, i):
+        k = d // 2
+        return remote(nears.at[k, i], nearr.at[k, i], sem_near.at[0, k, i], sem_near.at[1, k, i], xdev(d))
 
     def copy_o2(i, d):
         return remote(o2s.at[i, d - 1], o2r.at[i, d - 1], sem_o2.at[0, i, d - 1], sem_o2.at[1, i, d - 1], zdev(d))
 
-    for i in range(2):
-        n = 1 - kp if i == 0 else kp
-        for d in (2, 1, 3):
-            o1s[i, d - 1] = final(lax.rem(x + d, 4), n).astype(BF)
-            copy_o1(i, d).start()
-    mine = pl.ds(mult(x * 256, 256), 256)
-    for i in range(2):
-        n = 1 - kp if i == 0 else kp
-        acc[mine, pl.ds(mult(n * 512, 512), 512)] = final(x, n)
-
-    for i in range(2):
-        n = 1 - kp if i == 0 else kp
-        for d in (1, 3, 2):
-            copy_o1(i, d).wait_recv()
-
-        def summed(zs):
-            r = pl.ds(mult(zs * 64, 64), 64)
-            total = acc[pl.ds(mult(x * 256 + zs * 64, 64), 64), pl.ds(mult(n * 512, 512), 512)]
-            for d in range(3):
-                total = total + o1r[i, d, r, :].astype(F32)
-            return total
-
-        for d in (1, 3, 2):
-            o2s[i, d - 1] = summed(lax.rem(zl + d, 4)).astype(BF)
-            copy_o2(i, d).start()
-        own3[i] = summed(zl)
-
-    o3 = remote(o3s, out.at[pl.ds(mult(a * 64, 64), 64), :], sem_o3.at[0], sem_o3.at[1], dev_a)
-    for i in range(2):
+    def copy_o3(i):
+        rows = pl.ds(mult(a * 64, 64), 64)
+        return remote(o3s.at[i], out.at[rows, i * 256:(i + 1) * 256], sem_o3.at[0, i], sem_o3.at[1, i], dev_a)
+
+    for i in range(4):
+        fars[i] = final(lax.rem(x + 2, 4), i).astype(BF)
+        copy_far(i).start()
+    for i in range(4):
+        d = 3 if i % 2 == 0 else 1
+        nears[d // 2, i] = final(lax.rem(x + d, 4), i).astype(BF)
+        copy_near(d, i).start()
+    for i in range(4):
+        d = 1 if i % 2 == 0 else 3
+        mine = final(lax.rem(x + d, 4), i)
+        copy_far(i).wait_recv()
+        nears[d // 2, i] = (mine + farr[i].astype(F32)).astype(BF)
+        copy_near(d, i).start()
+    for i in range(4):
+        acc[pl.ds(mult(x * 256, 256), 256), pl.ds(columns(i), 256)] = final(x, i)
+
+    def finish(i):
         for d in (1, 3, 2):
             copy_o2(i, d).wait_recv()
         total = own3[i]
         for d in range(3):
             total = total + o2r[i, d].astype(F32)
-        if i == 0:
-            o3s[...] = total.astype(BF)
-            o3.start()
+        if i < 2:
+            o3s[i] = total.astype(BF)
+            copy_o3(i).start()
         else:
-            out[pl.ds(mult(a * 64, 64), 64), :] = total.astype(BF)
+            out[pl.ds(mult(a * 64, 64), 64), (i - 2) * 256:(i - 1) * 256] = total.astype(BF)
+
+    for i in range(4):
+        for d in (1, 3):
+            copy_near(d, i).wait_recv()
+
+        def summed(zs):
+            r = pl.ds(mult(zs * 64, 64), 64)
+            total = acc[pl.ds(mult(x * 256 + zs * 64, 64), 64), pl.ds(columns(i), 256)]
+            for k in range(2):
+                total = total + nearr[k, i, r, :].astype(F32)
+            return total
+
+        for d in (2, 1, 3):
+            o2s[i, d - 1] = summed(lax.rem(zl + d, 4)).astype(BF)
+            copy_o2(i, d).start()
+        own3[i] = summed(zl)
+        if i >= 2:
+            finish(i - 2)
+    finish(2)
+    finish(3)
 
     for copy in sends:
         copy.wait_send()
 
     @pl.loop(0, NCH)
     def _(p):
-        copy_b(p).wait_send()
+        for i in range(2):
+            copy_b(p, i).wait_send()
+        for n, (dev, half) in enumerate(wdests):
+            remote(comb.at[half * NCH + p], wr.at[p, g], sem_ws.at[p, n], sem_wr.at[p, g], dev).wait_send()
         copy_z(p).wait_send()
 
     for s in range(3):
         for n, q in ((0, q_me), (1, q_me), (2, q_me), (3, q_z), (4, q_z), (5, q_b), (6, q_bz)):
             hcopy(s, n, q, sib).wait_send()
+    for i in range(4):
+        copy_far(i).wait_send()
+        for d in (1, 3):
+            copy_near(d, i).wait_send()
+        for d in (1, 2, 3):
+            copy_o2(i, d).wait_send()
     for i in range(2):
-        for d in (1, 2, 3):
-            copy_o1(i, d).wait_send()
-            copy_o2(i, d).wait_send()
-    o3.wait_send()
-    arrived(out.at[pl.ds(mult((1 - a) * 64, 64), 64), :], sem_o3.at[1])
+        copy_o3(i).wait_send()
+        arrived(out.at[pl.ds(mult((1 - a) * 64, 64), 64), i * 256:(i + 1) * 256], sem_o3.at[1, i])
 
 
 def per_device(
     tokens, gate_vals, gate_scales, gate_rows, up_vals, up_scales, up_rows, down_vals, down_scales, down_rows
 ):
-    row = lax.axis_index("row")
-    col = lax.axis_index("col")
-    g = (row % 2) * 2 + (row // 2) % 2
-    comb = jnp.concatenate([gate_vals.reshape(14, 8, 4096), up_vals.reshape(14, 8, 4096)], axis=1)
     draw = down_vals.transpose(1, 0, 2).reshape(112, 4096)
-
-    lane = jnp.arange(128, dtype=jnp.int32)
-
-    def chunked(gate, up):
-        both = jnp.stack([gate.reshape(2, 7, 8), up.reshape(2, 7, 8)], axis=2).reshape(2, 7, 16)
-        return jnp.pad(jnp.tile(both, (1, 1, 8)), ((0, 0), (0, 1), (0, 0)))
-
-    where = chunked(gate_rows - row * 8, up_rows - row * 8) + 8 * (lane // 4)
-    tabs = jnp.concatenate([where.astype(F32), chunked(gate_scales, up_scales)], axis=1)
-    tabs = jnp.where(lane // 16 == g, tabs, 0.0)
-
-    rel = down_rows - col * 28
-    cc = rel // 14
-    rr = rel - cc * 14
-    piece = (rr >= 8).astype(jnp.int32) + (rr >= 12).astype(jnp.int32)
-    rl = rr - jnp.where(piece == 0, 0, jnp.where(piece == 1, 8, 12))
-    code = ((cc * 3 + piece) * 8 + jnp.arange(8, dtype=jnp.int32)[:, None]) * 8 + rl
-    code = jnp.pad(code.T.reshape(1, 112).astype(F32), ((0, 0), (0, 16)), constant_values=-1.0)
-    tabd = jnp.concatenate(
-        [code, jnp.pad(down_scales.T.reshape(1, 112), ((0, 0), (0, 16))), jnp.zeros((6, 128), F32)], axis=0
-    )
-
     vm = pl.BlockSpec(memory_space=pltpu.VMEM)
     hb = pl.BlockSpec(memory_space=pl.ANY)
     dma = pltpu.SemaphoreType.DMA
     return pl.pallas_call(
         kernel,
         out_shape=jax.ShapeDtypeStruct((128, 512), BF),
-        in_specs=[vm, hb, hb, vm, vm],
+        in_specs=[vm, hb, hb, hb] + [vm] * 6,
         out_specs=vm,
         scratch_shapes=[
+            pltpu.VMEM((2, 28, 4, 4096), BF),
+            pltpu.VMEM((14, 16, 4096), BF),
+            pltpu.VMEM((2, 16, 128), F32),
+            pltpu.VMEM((8, 128), F32),
             pltpu.VMEM((1024, 2048), BF),
             pltpu.VMEM((128, 512), BF),
             pltpu.VMEM((512, 512), BF),
@@ -488,30 +565,36 @@
             pltpu.VMEM((1024, 1792), BF),
             pltpu.VMEM((1792, 1024), BF),
             pltpu.VMEM((1024, 1024), F32),
-            pltpu.VMEM((2, 3, 256, 512), BF),
-            pltpu.VMEM((2, 3, 256, 512), BF),
-            pltpu.VMEM((2, 3, 64, 512), BF),
-            pltpu.VMEM((2, 3, 64, 512), BF),
-            pltpu.VMEM((2, 64, 512), F32),
-            pltpu.VMEM((64, 512), BF),
+            pltpu.VMEM((4, 256, 256), BF),
+            pltpu.VMEM((4, 256, 256), BF),
+            pltpu.VMEM((2, 4, 256, 256), BF),
+            pltpu.VMEM((2, 4, 256, 256), BF),
+            pltpu.VMEM((4, 3, 64, 256), BF),
+            pltpu.VMEM((4, 3, 64, 256), BF),
+            pltpu.VMEM((4, 64, 256), F32),
+            pltpu.VMEM((2, 64, 256), BF),
+            dma((2,)),
             dma((2, 4)),
             dma((2, 4, 4)),
             dma((9, 3)),
             dma((9, 4)),
             dma((3, 2)),
-            dma((2, NCH)),
+            dma((2, NCH, 2)),
             dma((2, NCH)),
             dma((3, 7)),
             dma((3, 8)),
-            dma((2, 2, 3)),
-            dma((2, 2, 3)),
-            dma((2,)),
+            dma((2, 4)),
+            dma((2, 2, 4)),
+            dma((2, 4, 3)),
+            dma((2, 2)),
         ],
         compiler_params=pltpu.CompilerParams(
             collective_id=0, has_side_effects=True, vmem_limit_bytes=62 * 1024 * 1024
         ),
         name="gated_layer",
-    )(tokens, comb, draw, tabs, tabd)
+    )(
+        tokens, gate_vals, up_vals, draw, gate_rows.T, gate_scales.T, up_rows.T, up_scales.T, down_rows, down_scales
+    )
 
 
 def solution(mesh):

time: 159 us -> 150 us (0.943); the launches traced: 159 us -> 148 us
  Pallas kernels: 151 us -> 146 us
  local copies, waits for them, and re-layouts: 5.04 us -> 1.57 us
  other arithmetic: 2.71 us -> 0 us
    pallas_call x1, Pallas kernels: 151 us -> 146 us  [per_device(): pl.pallas_call(kernel, out_shape=jax.ShapeDtypeStruct((128, 512), BF), in...]
    concatenate x2 -> x0, other arithmetic: 2.03 us -> none  [the longest x1 1.36 us: per_device(): jnp.concatenate([gate_vals.reshape(14, 8, 4096), up_vals.reshape(14, 8, 4...]
    reshape x3 -> x0, local copies, waits for them, and re-layouts: 2.01 us -> none  [the longest x1 1.72 us: per_device(): up_vals.reshape(14, 8, 4096)]
where the time goes in v2:
time: 150 us; the launch traced here: 148 us
  Pallas kernels  146 us (97%)
  local copies, waits for them, and re-layouts  1.57 us (1%)
    pallas_call x1, Pallas kernels, per_device(): pl.pallas_call(kernel, out_shape=jax.ShapeDtypeStruct((128, 512), BF), in...  146 us

profile of v2, /device:TPU:8, one launch (start us, length us, event | category | flops | bytes accessed | tf_op | source)
XLA Modules:
  0.0 147.9 jit_solution(7216149333864752232)
XLA Ops:
  0.0 146.3 %gated_layer.1 = bf16[128,512]{1,0:T(8,128)(2,1)} custom-call(bf16[128,512]{1,0:T(8,128)(2,1)} %tok.1, bf16[28,4,4096]{2,1,0:T(4,128)(2,1)} %graw.1, bf16[28,4,4096]{2,1,0:T(4,128)(2,1)} %uraw.1, bf16[112,4096]{1,0:T(8,128)(2,1)} %bitcast.7, s32[4,28]{1,0:T(4,128)} %bitcast.8, f32[4,28]{1,0:T(4,128)} %bitcast.9, s32[4,28]{1,0:T(4,128)} %bitcast.10, ...), custom_call_target="tpu_custom_call" | custom-call | tf_op jit(solution)/shard_map/gated_layer/pallas_call | solution.py:540
  146.3 1.6 %copy.12 = bf16[128,512]{1,0:T(8,128)(2,1)} copy(bf16[128,512]{1,0:T(8,128)(2,1)} %gated_layer.1) | data formatting | bytes 262144

commit v3 on v2

--- a/solution.py
+++ b/solution.py
@@ -29,7 +29,7 @@
     raw, comb, tabs, tabd, x_all, tst, p512, wr, tb, dr, td, panel,
     own, bsend, brecv, own2, zsend, zrecv, hn, hid, wd, acc,
     fars, farr, nears, nearr, o2s, o2r, own3, o3s,
-    sem_raw, sem_t, sem_tx, sem_ws, sem_wr, sem_d, sem_b, sem_z, sem_hs, sem_hr, sem_far, sem_near, sem_o2, sem_o3,
+    sem_raw, sem_t, sem_zh, sem_xh, sem_sx, sem_tx, sem_ws, sem_wr, sem_d, sem_b, sem_z, sem_hs, sem_hr, sem_far, sem_near, sem_o2, sem_o3,
 ):
     row = lax.axis_index("row")
     col = lax.axis_index("col")
@@ -89,6 +89,20 @@
 
     go(remote(tst.at[pl.ds(mult((1 - a) * 64, 64), 64), :],
               x_all.at[pl.ds(myrow, 64), pl.ds(mylane, 512)], sem_t.at[0, 0], sem_t.at[1, 0], dev_a))
+    other = mult(core * 1024 + (1 - kp) * 512, 512)
+
+    def part(xs, zs, k):
+        return x_all.at[pl.ds(mult((xs * 4 + zs) * 64, 64), 64), pl.ds(mylane if k == 0 else other, 512)]
+
+    def spread_own(k):
+        mine = part(x, zl, k)
+        for d in (1, 3, 2):
+            go(remote(mine, mine, sem_zh.at[0, k, d], sem_zh.at[1, k, d], zdev(d)))
+        for d in (1, 3):
+            go(remote(mine, mine, sem_xh.at[0, k, d], sem_xh.at[1, k, d], xdev(d)))
+
+    spread_own(0)
+
     lane = lax.broadcasted_iota(jnp.int32, (8, 128), 1)
     sub = lax.broadcasted_iota(jnp.int32, (8, 128), 0)
     low = lane < 64
@@ -160,10 +174,8 @@
     def quarter(xs):
         return x_all.at[pl.ds(mult(xs * 256, 256), 256), pl.ds(corelane, 1024)]
 
-    other = mult(core * 1024 + (1 - kp) * 512, 512)
     arrived(x_all.at[pl.ds(myrow, 64), pl.ds(other, 512)], sem_t.at[1, 0])
-    for d in (1, 3, 2):
-        go(remote(block(x, zl), block(x, zl), sem_t.at[0, d], sem_t.at[1, d], zdev(d)))
+    spread_own(1)
 
     def along_x(zs, dz):
         for d in (1, 3):
@@ -171,16 +183,25 @@
 
     def from_z(dz):
         zs = lax.rem(zl + 4 - dz, 4)
-        arrived(block(x, zs), sem_t.at[1, dz])
+        for k in range(2):
+            arrived(part(x, zs, k), sem_zh.at[1, k, dz])
         along_x(zs, dz)
+
+    def from_x(d, dz):
+        xs, zs = lax.rem(x + 4 - d, 4), lax.rem(zl + 4 - dz, 4)
+        if dz == 0 and d != 2:
+            for k in range(2):
+                arrived(part(xs, zs, k), sem_xh.at[1, k, d])
+        else:
+            arrived(block(xs, zs), sem_tx.at[1, d, dz])
 
     def onward(dz):
         d = 1 if dz % 2 == 0 else 3
-        source = block(lax.rem(x + 4 - d, 4), lax.rem(zl + 4 - dz, 4))
-        arrived(source, sem_tx.at[1, d, dz])
+        xs, zs = lax.rem(x + 4 - d, 4), lax.rem(zl + 4 - dz, 4)
+        source = block(xs, zs)
+        from_x(d, dz)
         go(remote(source, source, sem_tx.at[0, 2, dz], sem_tx.at[1, 2, dz], xdev(d)))
 
-    along_x(zl, 0)
     send_weights()
     from_z(1)
     onward(0)
@@ -235,16 +256,24 @@
     def _(p):
         build(p)
 
-    for d in (1, 3, 2):
+    for d, waits in ((1, (1, 3)), (3, (0, 2))):
         xs = lax.rem(x + 4 - d, 4)
-        waits = {1: (1, 3), 3: (0, 2), 2: (0, 1, 2, 3)}[d]
         for dz in waits:
-            arrived(block(xs, lax.rem(zl + 4 - dz, 4)), sem_tx.at[1, d, dz])
+            from_x(d, dz)
         go(remote(quarter(xs), quarter(xs), sem_tx.at[0, 0, d], sem_tx.at[1, 0, d], sib))
+    xs = lax.rem(x + 2, 4)
+    for dz in (0, 1, 3, 2):
+        from_x(2, dz)
+        far = block(xs, lax.rem(zl + 4 - dz, 4))
+        go(remote(far, far, sem_sx.at[0, dz], sem_sx.at[1, dz], sib))
     siblane = mult((1 - core) * 1024, 1024)
-    for d in (0, 1, 3, 2):
+    for d in (0, 1, 3):
         xs = lax.rem(x + 4 - d, 4)
         arrived(x_all.at[pl.ds(mult(xs * 256, 256), 256), pl.ds(siblane, 1024)], sem_tx.at[1, 0, d])
+    xs = lax.rem(x + 2, 4)
+    for dz in range(4):
+        zs = lax.rem(zl + 4 - dz, 4)
+        arrived(x_all.at[pl.ds(mult((xs * 4 + zs) * 64, 64), 64), pl.ds(siblane, 1024)], sem_sx.at[1, dz])
 
     def product(p):
         def tokens_quarter(q):
@@ -575,6 +604,9 @@
             pltpu.VMEM((2, 64, 256), BF),
             dma((2,)),
             dma((2, 4)),
+            dma((2, 2, 4)),
+            dma((2, 2, 4)),
+            dma((2, 4)),
             dma((2, 4, 4)),
             dma((9, 3)),
             dma((9, 4)),

time: 150 us -> 150 us (level)
  no operation moved by 1% of the time
where the time goes in v3:
time: 150 us; the launch traced here: 148 us
  Pallas kernels  147 us (98%)
  local copies, waits for them, and re-layouts  1.57 us (1%)
    pallas_call x1, Pallas kernels, per_device(): pl.pallas_call(kernel, out_shape=jax.ShapeDtypeStruct((128, 512), BF), in...  147 us

profile of v3, /device:TPU:8, one launch (start us, length us, event | category | flops | bytes accessed | tf_op | source)
XLA Modules:
  0.0 148.2 jit_solution(3965885507632190135)
XLA Ops:
  0.0 146.6 %gated_layer.1 = bf16[128,512]{1,0:T(8,128)(2,1)} custom-call(bf16[128,512]{1,0:T(8,128)(2,1)} %tok.1, bf16[28,4,4096]{2,1,0:T(4,128)(2,1)} %graw.1, bf16[28,4,4096]{2,1,0:T(4,128)(2,1)} %uraw.1, bf16[112,4096]{1,0:T(8,128)(2,1)} %bitcast.7, s32[4,28]{1,0:T(4,128)} %bitcast.8, f32[4,28]{1,0:T(4,128)} %bitcast.9, s32[4,28]{1,0:T(4,128)} %bitcast.10, ...), custom_call_target="tpu_custom_call" | custom-call | tf_op jit(solution)/shard_map/gated_layer/pallas_call | solution.py:569
  146.6 1.6 %copy.12 = bf16[128,512]{1,0:T(8,128)(2,1)} copy(bf16[128,512]{1,0:T(8,128)(2,1)} %gated_layer.1) | data formatting | bytes 262144

commit v4 on v3

--- a/solution.py
+++ b/solution.py
@@ -247,14 +247,10 @@
                             jnp.concatenate(parts, axis=0).astype(BF)
                         )
 
-    EARLY = 3
+    EARLY = 1
     build(0)
     onward(3)
     onward(2)
-
-    @pl.loop(1, EARLY)
-    def _(p):
-        build(p)
 
     for d, waits in ((1, (1, 3)), (3, (0, 2))):
         xs = lax.rem(x + 4 - d, 4)
@@ -410,10 +406,6 @@
     def _(p):
         @pl.when(p < NCH)
         def _():
-            @pl.when(p >= EARLY)
-            def _():
-                build(p)
-
             product(p)
 
         @pl.when(p == 7)
@@ -423,6 +415,10 @@
         @pl.when(jnp.logical_and(p >= 1, p <= NCH))
         def _():
             add_b(p - 1)
+
+        @pl.when(p < NCH - 1)
+        def _():
+            build(p + 1)
 
         @pl.when(p >= 3)
         def _():

time: 150 us -> 150 us (level)
  no operation moved by 1% of the time
where the time goes in v4:
time: 150 us; the launch traced here: 149 us
  Pallas kernels  147 us (98%)
  local copies, waits for them, and re-layouts  1.57 us (1%)
    pallas_call x1, Pallas kernels, per_device(): pl.pallas_call(kernel, out_shape=jax.ShapeDtypeStruct((128, 512), BF), in...  147 us

profile of v4, /device:TPU:8, one launch (start us, length us, event | category | flops | bytes accessed | tf_op | source)
XLA Modules:
  0.0 148.9 jit_solution(12980683872784550895)
XLA Ops:
  0.0 147.3 %gated_layer.1 = bf16[128,512]{1,0:T(8,128)(2,1)} custom-call(bf16[128,512]{1,0:T(8,128)(2,1)} %tok.1, bf16[28,4,4096]{2,1,0:T(4,128)(2,1)} %graw.1, bf16[28,4,4096]{2,1,0:T(4,128)(2,1)} %uraw.1, bf16[112,4096]{1,0:T(8,128)(2,1)} %bitcast.7, s32[4,28]{1,0:T(4,128)} %bitcast.8, f32[4,28]{1,0:T(4,128)} %bitcast.9, s32[4,28]{1,0:T(4,128)} %bitcast.10, ...), custom_call_target="tpu_custom_call" | custom-call | tf_op jit(solution)/shard_map/gated_layer/pallas_call | solution.py:565
  147.3 1.6 %copy.12 = bf16[128,512]{1,0:T(8,128)(2,1)} copy(bf16[128,512]{1,0:T(8,128)(2,1)} %gated_layer.1) | data formatting | bytes 262144
